TPU v7x, 32 devices: a whole 2x2x4 slice. The times are simulated.
32 devices in a mesh: ctx: 8 (over z, x), head: 4 (over y, core).
Axes of the slice: x: 2, y: 2, z: 4, core: 2. Of those that a mesh axis runs over, the one named last changes fastest.
Arguments:
- query: bfloat16 [16384, 8192], P(('ctx', 'head')), as said below
- key: bfloat16 [16384, 1024], P(('ctx', 'head')), as said below
- value: bfloat16 [16384, 1024], P(('ctx', 'head')), may hold values from -6 to 6
- doc_ids: int32 [128], replicated, may hold values from 0 to 20, never falling along the last dimension, each value on 1 to 8 neighbouring positions
- plan: int32 [128], replicated, may hold values from 0 to 127, as said below
Outputs:
- attended: bfloat16 [16384, 8192], P('ctx', 'head')
Inputs may be any that keep to these rules, and one draw needn't show every extreme that they name: `doc_ids`: block ids never fall; each document holds 1 to 8 blocks, one exactly 8. `plan`: A permutation of the 128 blocks. Output positions k * 16 to (k + 1) * 16 - 1 belong to context shard k. Every shard receives 16 blocks; of the blocks j * 16 to (j + 1) * 16 - 1 at most 2 go to one shard, and exactly 2 to some shard. `query`: real values; no structure promised. `key`: real values; no structure promised.
All inputs are finite; a program needn't handle non-finite values.
Results may differ from a plain program's by a relative error of at most 0.0038.
Values may be sent and summed in bfloat16 or wider, within the bound.
A program may use at most 128 MiB of HBM per device.

v0:
```python
import functools
import math

import jax
import jax.numpy as jnp
from jax import lax
from jax.experimental import pallas as pl
from jax.experimental.pallas import tpu as pltpu
from jax.sharding import PartitionSpec as P

HD = 128
BLK = 128
MAXDOC = 8
HALO = (MAXDOC - 1) * BLK
MESH = pl.DeviceIdType.MESH


def aligned(x):
    return pl.multiple_of(x, BLK)


def fused_kernel(
    kv_heads, cap, slot_block, slot_count, q_ref, k_ref, v_ref, got_ref, *rest
):
    keys_in = rest[:kv_heads]
    values_in = rest[kv_heads : 2 * kv_heads]
    q_in, q_work, turned, v_work, out = rest[2 * kv_heads : 2 * kv_heads + 5]
    sems = rest[2 * kv_heads + 5 :]
    q_sent, q_got, kv_sent, kv_got, halo_sent, halo_got, out_sent, out_got, own_done = sems
    c, h = lax.axis_index("ctx"), lax.axis_index("head")
    nc, nh = lax.axis_size("ctx"), lax.axis_size("head")
    part = q_ref.shape[0]
    rows = nh * part
    blocks = rows // BLK
    heads = q_in.shape[0]
    group = heads // kv_heads
    factor = math.log2(math.e) / math.sqrt(HD)

    barrier = pltpu.get_barrier_semaphore()
    for d in range(1, nh):
        pl.semaphore_signal(
            barrier, inc=1, device_id=(c, lax.rem(h + d, nh)), device_id_type=MESH
        )
    for d in range(1, nc):
        pl.semaphore_signal(
            barrier, inc=1, device_id=(lax.rem(c + d, nc), h), device_id_type=MESH
        )
    pl.semaphore_wait(barrier, nh + nc - 2)

    my_rows = pl.ds(aligned(h * part), part)
    my_kv_rows = pl.ds(aligned(HALO + h * part), part)

    def send_kv(g):
        for at, (src, dst) in enumerate(((k_ref, keys_in[g]), (v_ref, values_in[g]))):
            for d in range(1, nh):
                t = lax.rem(h + d, nh)
                pltpu.make_async_remote_copy(
                    src_ref=src.at[:, pl.ds(aligned((t * kv_heads + g) * HD), HD)],
                    dst_ref=dst.at[my_kv_rows],
                    send_sem=kv_sent.at[g, at, d],
                    recv_sem=kv_got.at[g, at, h],
                    device_id=(c, t),
                    device_id_type=MESH,
                ).start()
            pltpu.make_async_copy(
                src.at[:, pl.ds(aligned((h * kv_heads + g) * HD), HD)],
                dst.at[my_kv_rows],
                kv_got.at[g, at, h],
            ).start()

    def send_q(k):
        for d in range(1, nh):
            t = lax.rem(h + d, nh)
            pltpu.make_async_remote_copy(
                src_ref=q_ref.at[:, pl.ds(aligned((t * heads + k) * HD), HD)],
                dst_ref=q_in.at[k, my_rows],
                send_sem=q_sent.at[k, d],
                recv_sem=q_got.at[k, h],
                device_id=(c, t),
                device_id_type=MESH,
            ).start()
        pltpu.make_async_copy(
            q_ref.at[:, pl.ds(aligned((h * heads + k) * HD), HD)],
            q_in.at[k, my_rows],
            q_got.at[k, h],
        ).start()

    def wait_on(ref, sem):
        pltpu.make_async_copy(ref, ref, sem).wait()

    def send_q_loop(k, carry):
        send_q(k)
        return carry

    send_kv(0)
    send_q(0)
    for g in range(1, kv_heads):
        send_kv(g)
    lax.fori_loop(1, heads, send_q_loop, 0)

    pieces = []
    for j in range(nh - 1, -1, -1):
        low, high = max(rows - HALO, j * part), (j + 1) * part
        if low < high:
            pieces.append((j, low, high - low))

    def halo_copy(g, at, p):
        ref = (keys_in[g], values_in[g])[at]
        _, low, size = pieces[p]
        return pltpu.make_async_remote_copy(
            src_ref=ref.at[pl.ds(HALO + low, size)],
            dst_ref=ref.at[pl.ds(HALO + low - rows, size)],
            send_sem=halo_sent.at[g, at, p],
            recv_sem=halo_got.at[g, at, p],
            device_id=(jnp.minimum(c + 1, nc - 1), h),
            device_id_type=MESH,
        )

    def gather_kv(g):
        waited = set()

        def wait_part(at, j):
            if (at, j) not in waited:
                waited.add((at, j))
                ref = (keys_in[g], values_in[g])[at]
                wait_on(ref.at[pl.ds(HALO + j * part, part)], kv_got.at[g, at, j])

        for at in range(2):
            for p in range(len(pieces)):
                wait_part(at, pieces[p][0])

                @pl.when(c < nc - 1)
                def _():
                    halo_copy(g, at, p).start()

        for at in range(2):
            for j in range(nh):
                wait_part(at, j)

    def turn(g, first, last):
        for i in range(first, last):
            turned[i] = keys_in[g][i * BLK : (i + 1) * BLK, :].T

    def finish_kv(g):
        turn(g, MAXDOC - 1, MAXDOC - 1 + blocks)

        @pl.when(c > 0)
        def _():
            for at in range(2):
                for p in range(len(pieces)):
                    halo_copy(g, at, p).wait_recv()

        @pl.when(c == 0)
        def _():
            for ref in (keys_in[g], values_in[g]):
                ref[0:HALO, :] = jnp.zeros((HALO, HD), ref.dtype)

        turn(g, 0, MAXDOC - 1)
        v_work[...] = values_in[g][...].reshape(v_work.shape)

    causal = lax.broadcasted_iota(jnp.int32, (BLK, BLK), 1) <= lax.broadcasted_iota(
        jnp.int32, (BLK, BLK), 0
    )

    def attend(g, k, slot):
        block = slot_block[slot]
        count = slot_count[slot]
        queries = q_work[block]
        keys = jnp.concatenate([turned[block + i] for i in range(MAXDOC)], axis=1)
        values = jnp.concatenate([v_work[block + i] for i in range(MAXDOC)], axis=0)
        scores = jnp.dot(queries, keys, preferred_element_type=jnp.float32)
        parts = [scores[:, i * BLK : (i + 1) * BLK] for i in range(MAXDOC)]
        for i in range(MAXDOC - 1):
            inside = jnp.full((BLK, BLK), count - (MAXDOC - 1 - i), jnp.int32) > 0
            parts[i] = jnp.where(inside, parts[i], -jnp.inf)
        parts[-1] = jnp.where(causal, parts[-1], -jnp.inf)
        top = jnp.max(functools.reduce(jnp.maximum, parts), axis=1, keepdims=True)
        parts = [jnp.exp2((x - top) * factor) for x in parts]
        total = jnp.sum(functools.reduce(jnp.add, parts), axis=1, keepdims=True)
        weights = jnp.concatenate([x.astype(jnp.bfloat16) for x in parts], axis=1)
        mixed = jnp.dot(weights, values, preferred_element_type=jnp.float32) / total
        out[k, slot] = mixed.astype(out.dtype)

    def columns(k):
        return pl.ds(aligned(k * HD), HD)

    def send_out(k, d):
        t = lax.rem(c + d, nc)
        pltpu.make_async_remote_copy(
            src_ref=out.at[k, pl.ds(t * cap, cap)],
            dst_ref=got_ref.at[pl.ds(c * cap, cap), :, columns(k)],
            send_sem=out_sent.at[k],
            recv_sem=out_got.at[k],
            device_id=(t, h),
            device_id_type=MESH,
        ).start()

    def own_copy(k):
        mine = pl.ds(c * cap, cap)
        return pltpu.make_async_copy(
            out.at[k, mine], got_ref.at[mine, :, columns(k)], own_done.at[k]
        )

    def head_step(g, k):
        for j in range(nh):
            wait_on(q_in.at[k, pl.ds(j * part, part)], q_got.at[k, j])
        q_work[...] = q_in[k].reshape(q_work.shape)

        def target(d, carry):
            t = lax.rem(c + d, nc)
            for r in range(cap):
                attend(g, k, t * cap + r)

            @pl.when(d > 1)
            def _():
                send_out(k, d - 1)

            return carry

        lax.fori_loop(1, nc + 1, target, 0)
        own_copy(k).start()

    gather_kv(0)
    for g in range(kv_heads):
        finish_kv(g)

        def one(k, carry, g=g):
            head_step(g, k)
            return carry

        lax.fori_loop(g * group, g * group + 1, one, 0)
        if g + 1 < kv_heads:
            gather_kv(g + 1)
        lax.fori_loop(g * group + 1, (g + 1) * group, one, 0)

    for g in range(kv_heads):
        for at in range(2):
            for d in range(1, nh):
                wait_on(keys_in[g].at[my_kv_rows], kv_sent.at[g, at, d])

            @pl.when(c < nc - 1)
            def _():
                for p in range(len(pieces)):
                    halo_copy(g, at, p).wait_send()

    def drain(k, carry):
        for d in range(1, nh):
            wait_on(q_in.at[k, my_rows], q_sent.at[k, d])
        own_copy(k).wait()
        wait_on(out.at[k, pl.ds(0, (nc - 1) * cap)], out_sent.at[k])
        wait_on(got_ref.at[pl.ds(0, (nc - 1) * cap), :, columns(k)], out_got.at[k])
        return carry

    lax.fori_loop(0, heads, drain, 0)


def fused(slot_block, slot_count, query, key, value):
    nc, nh = lax.axis_size("ctx"), lax.axis_size("head")
    part = query.shape[0]
    rows = nh * part
    heads = query.shape[1] // nh // HD
    kv_heads = key.shape[1] // nh // HD
    cap = -(-(rows // BLK) // nc)
    slots = nc * cap
    window = HALO + rows
    dma = pltpu.SemaphoreType.DMA
    return pl.pallas_call(
        functools.partial(fused_kernel, kv_heads, cap),
        out_shape=jax.ShapeDtypeStruct((slots, BLK, heads * HD), query.dtype),
        in_specs=[pl.BlockSpec(memory_space=pltpu.SMEM)] * 2
        + [pl.BlockSpec(memory_space=pl.ANY)] * 3,
        out_specs=pl.BlockSpec(memory_space=pl.ANY),
        scratch_shapes=[pltpu.VMEM((window, HD), query.dtype)] * (2 * kv_heads)
        + [
            pltpu.VMEM((heads, rows, HD), query.dtype),
            pltpu.VMEM((rows // BLK, BLK, HD), query.dtype),
            pltpu.VMEM((window // BLK, HD, BLK), query.dtype),
            pltpu.VMEM((window // BLK, BLK, HD), query.dtype),
            pltpu.VMEM((heads, slots, BLK, HD), query.dtype),
            dma((heads, nh)),
            dma((heads, nh)),
            dma((kv_heads, 2, nh)),
            dma((kv_heads, 2, nh)),
            dma((kv_heads, 2, nh)),
            dma((kv_heads, 2, nh)),
            dma((heads,)),
            dma((heads,)),
            dma((heads,)),
        ],
        compiler_params=pltpu.CompilerParams(collective_id=0, has_side_effects=True),
        name="fused",
    )(slot_block, slot_count, query, key, value)


def prepare_kernel(blocks, cap, doc_ref, plan_ref, slot_block, slot_count, mine):
    c, nc = lax.axis_index("ctx"), lax.axis_size("ctx")

    def table(k, carry):
        found = [jnp.int32(0)] * cap
        seen = jnp.int32(0)
        for i in range(blocks):
            p = plan_ref[k * blocks + i]
            hit = lax.div(p, blocks) == c
            for r in range(cap):
                found[r] = jnp.where(hit & (seen == r), lax.rem(p, blocks), found[r])
            seen = seen + jnp.where(hit, 1, 0)
        for r in range(cap):
            at = c * blocks + found[r]
            document = doc_ref[at]
            count = jnp.int32(1)
            for t in range(1, MAXDOC):
                same = doc_ref[jnp.maximum(at - t, 0)] == document
                count = count + jnp.where((at >= t) & same, 1, 0)
            slot_block[k * cap + r] = found[r]
            slot_count[k * cap + r] = count
        return carry

    lax.fori_loop(0, nc, table, 0)

    sources = [lax.div(plan_ref[c * blocks + i], blocks) for i in range(blocks)]
    for i in range(blocks):
        rank = jnp.int32(0)
        for before in range(i):
            rank = rank + jnp.where(sources[before] == sources[i], 1, 0)
        mine[i] = sources[i] * cap + jnp.minimum(rank, cap - 1)


def prepare(doc_ids, plan, blocks, cap):
    slots = lax.axis_size("ctx") * cap
    sizes = (slots, slots, blocks)
    return pl.pallas_call(
        functools.partial(prepare_kernel, blocks, cap),
        out_shape=[jax.ShapeDtypeStruct((n,), jnp.int32) for n in sizes],
        in_specs=[pl.BlockSpec(memory_space=pltpu.SMEM)] * 2,
        out_specs=[pl.BlockSpec(memory_space=pltpu.SMEM)] * 3,
        name="prepare",
    )(doc_ids, plan)


def place_kernel(mine_ref, got_ref, o_ref, stage, in_sems, out_sems):
    blocks = o_ref.shape[0] // BLK
    incoming = []
    for i in range(blocks):
        copy = pltpu.make_async_copy(got_ref.at[mine_ref[i]], stage.at[i], in_sems.at[i])
        copy.start()
        incoming.append(copy)
    outgoing = []
    for i in range(blocks):
        incoming[i].wait()
        copy = pltpu.make_async_copy(
            stage.at[i], o_ref.at[pl.ds(i * BLK, BLK)], out_sems.at[i]
        )
        copy.start()
        outgoing.append(copy)
    for copy in outgoing:
        copy.wait()


def place(mine, got):
    blocks = mine.shape[0]
    width = got.shape[2]
    return pl.pallas_call(
        place_kernel,
        out_shape=jax.ShapeDtypeStruct((blocks * BLK, width), got.dtype),
        in_specs=[
            pl.BlockSpec(memory_space=pltpu.SMEM),
            pl.BlockSpec(memory_space=pl.ANY),
        ],
        out_specs=pl.BlockSpec(memory_space=pl.ANY),
        scratch_shapes=[
            pltpu.VMEM((blocks, BLK, width), got.dtype),
            pltpu.SemaphoreType.DMA((blocks,)),
            pltpu.SemaphoreType.DMA((blocks,)),
        ],
        name="place",
    )(mine, got)


def shards(query, key, value, doc_ids, plan):
    blocks = lax.axis_size("head") * query.shape[0] // BLK
    cap = -(-blocks // lax.axis_size("ctx"))
    slot_block, slot_count, mine = prepare(doc_ids, plan, blocks, cap)
    return place(mine, fused(slot_block, slot_count, query, key, value))


def solution(mesh):
    return jax.shard_map(
        shards,
        mesh=mesh,
        in_specs=(
            P(("ctx", "head"), None),
            P(("ctx", "head"), None),
            P(("ctx", "head"), None),
            P(),
            P(),
        ),
        out_specs=P("ctx", "head"),
        check_vma=False,
    )
```

profile of v0, /device:TPU:21, one launch (start us, length us, event | category | flops | bytes accessed | tf_op | source)
XLA Modules:
  0.0 223.9 jit_solution(8995659022839498313)
XLA Ops:
  0.0 2.4 %prepare.1 = (s32[16]{0:T(128)}, s32[16]{0:T(128)}, s32[16]{0:T(128)}) custom-call(s32[128]{0:T(128)} %doc_ref.1, s32[128]{0:T(128)} %plan_ref.1), custom_call_target="tpu_custom_call" | custom-call | tf_op jit(solution)/shard_map/prepare/pallas_call | solution.py:331
  2.4 214.2 %fused.1.got_ref = bf16[16,128,2048]{2,1,0:T(8,128)(2,1)} custom-call(s32[16]{0:T(128)} %get-tuple-element.9.slot_block, s32[16]{0:T(128)} %get-tuple-element.10.slot_count, bf16[512,8192]{1,0:T(8,128)(2,1)} %q_ref.1, bf16[512,1024]{1,0:T(8,128)(2,1)} %k_ref.1, bf16[512,1024]{1,0:T(8,128)(2,1)} %v_ref.1), custom_call_target="tpu_custom_call" | custom-call | tf_op jit(solution)/shard_map/fused/pallas_call | solution.py:267
  216.6 7.2 %place.1 = bf16[2048,2048]{1,0:T(8,128)(2,1)} custom-call(s32[16]{0:T(128)} %get-tuple-element.8.mine_ref, bf16[16,128,2048]{2,1,0:T(8,128)(2,1)} %fused.1.got_ref), custom_call_target="tpu_custom_call" | custom-call | tf_op jit(solution)/shard_map/place/pallas_call | solution.py:362
where the time goes:
time: 227 us; the launch traced here: 224 us
  Pallas kernels  224 us (99%)
    pallas_call x1, Pallas kernels, fused(): pl.pallas_call(functools.partial(fused_kernel, kv_heads, cap), out_shape=...  214 us
    pallas_call x1, Pallas kernels, place(): pl.pallas_call(place_kernel, out_shape=jax.ShapeDtypeStruct((blocks * BLK...  7.24 us

commit v1 on v0

v1 whole, which is shorter than its diff:
```python
import functools
import math

import jax
import jax.numpy as jnp
from jax import lax
from jax.experimental import pallas as pl
from jax.experimental.pallas import tpu as pltpu
from jax.sharding import PartitionSpec as P

HD = 128
BLK = 128
MAXDOC = 8
HALO = (MAXDOC - 1) * BLK
EARLY = 3
MESH = pl.DeviceIdType.MESH


def aligned(x):
    return pl.multiple_of(x, BLK)


def fused_kernel(
    kv_heads, cap, doc_ref, plan_ref, q_ref, k_ref, v_ref, got_ref, mine_ref, slot_block, slot_count, *rest
):
    keys_in = rest[:kv_heads]
    values_in = rest[kv_heads : 2 * kv_heads]
    q_in, q_work, turned, v_work, out = rest[2 * kv_heads : 2 * kv_heads + 5]
    sems = rest[2 * kv_heads + 5 :]
    q_sent, q_got, kv_sent, kv_got, halo_sent, halo_got, out_sent, out_got, own_done = sems
    c, h = lax.axis_index("ctx"), lax.axis_index("head")
    nc, nh = lax.axis_size("ctx"), lax.axis_size("head")
    part = q_ref.shape[0]
    rows = nh * part
    blocks = rows // BLK
    heads = q_in.shape[0]
    group = heads // kv_heads
    factor = math.log2(math.e) / math.sqrt(HD)

    barrier = pltpu.get_barrier_semaphore()
    for d in range(1, nh):
        pl.semaphore_signal(
            barrier, inc=1, device_id=(c, lax.rem(h + d, nh)), device_id_type=MESH
        )
    for d in range(1, nc):
        pl.semaphore_signal(
            barrier, inc=1, device_id=(lax.rem(c + d, nc), h), device_id_type=MESH
        )
    pl.semaphore_wait(barrier, nh + nc - 2)

    my_rows = pl.ds(aligned(h * part), part)
    my_kv_rows = pl.ds(aligned(HALO + h * part), part)

    def send_kv(g):
        for at, (src, dst) in enumerate(((k_ref, keys_in[g]), (v_ref, values_in[g]))):
            for d in range(1, nh):
                t = lax.rem(h + d, nh)
                pltpu.make_async_remote_copy(
                    src_ref=src.at[:, pl.ds(aligned((t * kv_heads + g) * HD), HD)],
                    dst_ref=dst.at[my_kv_rows],
                    send_sem=kv_sent.at[g, at, d],
                    recv_sem=kv_got.at[g, at, h],
                    device_id=(c, t),
                    device_id_type=MESH,
                ).start()
            pltpu.make_async_copy(
                src.at[:, pl.ds(aligned((h * kv_heads + g) * HD), HD)],
                dst.at[my_kv_rows],
                kv_got.at[g, at, h],
            ).start()

    def send_q(k):
        for d in range(1, nh):
            t = lax.rem(h + d, nh)
            pltpu.make_async_remote_copy(
                src_ref=q_ref.at[:, pl.ds(aligned((t * heads + k) * HD), HD)],
                dst_ref=q_in.at[k, my_rows],
                send_sem=q_sent.at[k, d],
                recv_sem=q_got.at[k, h],
                device_id=(c, t),
                device_id_type=MESH,
            ).start()
        pltpu.make_async_copy(
            q_ref.at[:, pl.ds(aligned((h * heads + k) * HD), HD)],
            q_in.at[k, my_rows],
            q_got.at[k, h],
        ).start()

    def wait_on(ref, sem):
        pltpu.make_async_copy(ref, ref, sem).wait()

    def send_q_loop(k, carry):
        send_q(k)
        return carry

    send_kv(0)
    sent = 0
    for g in range(1, kv_heads):
        upto = (g - 1) * group + EARLY
        lax.fori_loop(sent, upto, send_q_loop, 0)
        send_kv(g)
        sent = upto
    lax.fori_loop(sent, heads, send_q_loop, 0)

    def table(k, carry):
        found = [jnp.int32(0)] * cap
        seen = jnp.int32(0)
        for i in range(blocks):
            p = plan_ref[k * blocks + i]
            hit = lax.div(p, blocks) == c
            for r in range(cap):
                found[r] = jnp.where(hit & (seen == r), lax.rem(p, blocks), found[r])
            seen = seen + jnp.where(hit, 1, 0)
        for r in range(cap):
            at = c * blocks + found[r]
            document = doc_ref[at]
            count = jnp.int32(1)
            for t in range(1, MAXDOC):
                same = doc_ref[jnp.maximum(at - t, 0)] == document
                count = count + jnp.where((at >= t) & same, 1, 0)
            slot_block[k * cap + r] = found[r]
            slot_count[k * cap + r] = count
        return carry

    lax.fori_loop(0, nc, table, 0)

    sources = [lax.div(plan_ref[c * blocks + i], blocks) for i in range(blocks)]
    for i in range(blocks):
        rank = jnp.int32(0)
        for before in range(i):
            rank = rank + jnp.where(sources[before] == sources[i], 1, 0)
        mine_ref[i] = sources[i] * cap + jnp.minimum(rank, cap - 1)

    pieces = []
    for j in range(nh - 1, -1, -1):
        low, high = max(rows - HALO, j * part), (j + 1) * part
        if low < high:
            pieces.append((j, low, high - low))

    def halo_copy(g, at, p):
        ref = (keys_in[g], values_in[g])[at]
        _, low, size = pieces[p]
        return pltpu.make_async_remote_copy(
            src_ref=ref.at[pl.ds(HALO + low, size)],
            dst_ref=ref.at[pl.ds(HALO + low - rows, size)],
            send_sem=halo_sent.at[g, at, p],
            recv_sem=halo_got.at[g, at, p],
            device_id=(jnp.minimum(c + 1, nc - 1), h),
            device_id_type=MESH,
        )

    def gather_kv(g):
        waited = set()

        def wait_part(at, j):
            if (at, j) not in waited:
                waited.add((at, j))
                ref = (keys_in[g], values_in[g])[at]
                wait_on(ref.at[pl.ds(HALO + j * part, part)], kv_got.at[g, at, j])

        for at in range(2):
            for p in range(len(pieces)):
                wait_part(at, pieces[p][0])

                @pl.when(c < nc - 1)
                def _():
                    halo_copy(g, at, p).start()

        for at in range(2):
            for j in range(nh):
                wait_part(at, j)

    def turn(g, first, last):
        for i in range(first, last):
            turned[i] = keys_in[g][i * BLK : (i + 1) * BLK, :].T

    def finish_kv(g):
        turn(g, MAXDOC - 1, MAXDOC - 1 + blocks)

        @pl.when(c > 0)
        def _():
            for at in range(2):
                for p in range(len(pieces)):
                    halo_copy(g, at, p).wait_recv()

        @pl.when(c == 0)
        def _():
            for ref in (keys_in[g], values_in[g]):
                ref[0:HALO, :] = jnp.zeros((HALO, HD), ref.dtype)

        turn(g, 0, MAXDOC - 1)
        v_work[...] = values_in[g][...].reshape(v_work.shape)

    causal = lax.broadcasted_iota(jnp.int32, (BLK, BLK), 1) <= lax.broadcasted_iota(
        jnp.int32, (BLK, BLK), 0
    )

    def attend(g, k, slot):
        block = slot_block[slot]
        count = slot_count[slot]
        queries = q_work[block]
        keys = jnp.concatenate([turned[block + i] for i in range(MAXDOC)], axis=1)
        values = jnp.concatenate([v_work[block + i] for i in range(MAXDOC)], axis=0)
        scores = jnp.dot(queries, keys, preferred_element_type=jnp.float32)
        parts = [scores[:, i * BLK : (i + 1) * BLK] for i in range(MAXDOC)]
        for i in range(MAXDOC - 1):
            inside = jnp.full((BLK, BLK), count - (MAXDOC - 1 - i), jnp.int32) > 0
            parts[i] = jnp.where(inside, parts[i], -jnp.inf)
        parts[-1] = jnp.where(causal, parts[-1], -jnp.inf)
        top = jnp.max(functools.reduce(jnp.maximum, parts), axis=1, keepdims=True)
        parts = [jnp.exp2((x - top) * factor) for x in parts]
        total = jnp.sum(functools.reduce(jnp.add, parts), axis=1, keepdims=True)
        weights = jnp.concatenate([x.astype(jnp.bfloat16) for x in parts], axis=1)
        mixed = jnp.dot(weights, values, preferred_element_type=jnp.float32) / total
        out[k, slot] = mixed.astype(out.dtype)

    def columns(k):
        return pl.ds(aligned(k * HD), HD)

    def send_out(k, d):
        t = lax.rem(c + d, nc)
        pltpu.make_async_remote_copy(
            src_ref=out.at[k, pl.ds(t * cap, cap)],
            dst_ref=got_ref.at[pl.ds(c * cap, cap), :, columns(k)],
            send_sem=out_sent.at[k],
            recv_sem=out_got.at[k],
            device_id=(t, h),
            device_id_type=MESH,
        ).start()

    def own_copy(k):
        mine = pl.ds(c * cap, cap)
        return pltpu.make_async_copy(
            out.at[k, mine], got_ref.at[mine, :, columns(k)], own_done.at[k]
        )

    def head_step(g, k):
        for j in range(nh):
            wait_on(q_in.at[k, pl.ds(j * part, part)], q_got.at[k, j])
        q_work[...] = q_in[k].reshape(q_work.shape)

        def target(d, carry):
            t = lax.rem(c + d, nc)
            for r in range(cap):
                attend(g, k, t * cap + r)

            @pl.when(d > 1)
            def _():
                send_out(k, d - 1)

            return carry

        lax.fori_loop(1, nc + 1, target, 0)
        own_copy(k).start()

    gather_kv(0)
    for g in range(kv_heads):
        finish_kv(g)

        def one(k, carry, g=g):
            head_step(g, k)
            return carry

        lax.fori_loop(g * group, g * group + EARLY, one, 0)
        if g + 1 < kv_heads:
            gather_kv(g + 1)
        lax.fori_loop(g * group + EARLY, (g + 1) * group, one, 0)

    for g in range(kv_heads):
        for at in range(2):
            for d in range(1, nh):
                wait_on(keys_in[g].at[my_kv_rows], kv_sent.at[g, at, d])

            @pl.when(c < nc - 1)
            def _():
                for p in range(len(pieces)):
                    halo_copy(g, at, p).wait_send()

    def drain(k, carry):
        for d in range(1, nh):
            wait_on(q_in.at[k, my_rows], q_sent.at[k, d])
        own_copy(k).wait()
        wait_on(out.at[k, pl.ds(0, (nc - 1) * cap)], out_sent.at[k])
        wait_on(got_ref.at[pl.ds(0, (nc - 1) * cap), :, columns(k)], out_got.at[k])
        return carry

    lax.fori_loop(0, heads, drain, 0)


def fused(doc_ids, plan, query, key, value):
    nc, nh = lax.axis_size("ctx"), lax.axis_size("head")
    part = query.shape[0]
    rows = nh * part
    heads = query.shape[1] // nh // HD
    kv_heads = key.shape[1] // nh // HD
    cap = -(-(rows // BLK) // nc)
    slots = nc * cap
    window = HALO + rows
    dma = pltpu.SemaphoreType.DMA
    elements = (2 * kv_heads + 2) * window + (heads + 1) * rows + heads * slots * BLK
    held = 2 * elements * HD
    return pl.pallas_call(
        functools.partial(fused_kernel, kv_heads, cap),
        out_shape=[
            jax.ShapeDtypeStruct((slots, BLK, heads * HD), query.dtype),
            jax.ShapeDtypeStruct((rows // BLK,), jnp.int32),
        ],
        in_specs=[pl.BlockSpec(memory_space=pltpu.SMEM)] * 2
        + [pl.BlockSpec(memory_space=pltpu.HBM)] * 3,
        out_specs=[
            pl.BlockSpec(memory_space=pl.ANY),
            pl.BlockSpec(memory_space=pltpu.SMEM),
        ],
        scratch_shapes=[pltpu.SMEM((slots,), jnp.int32)] * 2
        + [pltpu.VMEM((window, HD), query.dtype)] * (2 * kv_heads)
        + [
            pltpu.VMEM((heads, rows, HD), query.dtype),
            pltpu.VMEM((rows // BLK, BLK, HD), query.dtype),
            pltpu.VMEM((window // BLK, HD, BLK), query.dtype),
            pltpu.VMEM((window // BLK, BLK, HD), query.dtype),
            pltpu.VMEM((heads, slots, BLK, HD), query.dtype),
            dma((heads, nh)),
            dma((heads, nh)),
            dma((kv_heads, 2, nh)),
            dma((kv_heads, 2, nh)),
            dma((kv_heads, 2, nh)),
            dma((kv_heads, 2, nh)),
            dma((heads,)),
            dma((heads,)),
            dma((heads,)),
        ],
        compiler_params=pltpu.CompilerParams(
            collective_id=0, has_side_effects=True, vmem_limit_bytes=held + (6 << 20)
        ),
        name="fused",
    )(doc_ids, plan, query, key, value)


def place_kernel(mine_ref, got_ref, o_ref, sems):
    copies = []
    for i in range(o_ref.shape[0] // BLK):
        copy = pltpu.make_async_copy(
            got_ref.at[mine_ref[i]], o_ref.at[pl.ds(i * BLK, BLK)], sems.at[i]
        )
        copy.start()
        copies.append(copy)
    for copy in copies:
        copy.wait()


def place(mine, got):
    blocks = mine.shape[0]
    width = got.shape[2]
    return pl.pallas_call(
        place_kernel,
        out_shape=jax.ShapeDtypeStruct((blocks * BLK, width), got.dtype),
        in_specs=[
            pl.BlockSpec(memory_space=pltpu.SMEM),
            pl.BlockSpec(memory_space=pl.ANY),
        ],
        out_specs=pl.BlockSpec(memory_space=pl.ANY),
        scratch_shapes=[pltpu.SemaphoreType.DMA((blocks,))],
        compiler_params=pltpu.CompilerParams(vmem_limit_bytes=1 << 20),
        name="place",
    )(mine, got)


def shards(query, key, value, doc_ids, plan):
    operands = [
        pltpu.with_memory_space_constraint(x, pltpu.HBM)
        for x in (doc_ids, plan, query, key, value)
    ]
    got, mine = fused(*operands)
    return place(mine, got)


def solution(mesh):
    return jax.shard_map(
        shards,
        mesh=mesh,
        in_specs=(
            P(("ctx", "head"), None),
            P(("ctx", "head"), None),
            P(("ctx", "head"), None),
            P(),
            P(),
        ),
        out_specs=P("ctx", "head"),
        check_vma=False,
    )
```

time: 227 us -> 221 us (0.974)
  Pallas kernels: 224 us -> 219 us
    pallas_call x1, Pallas kernels: 7.24 us -> 3.96 us  [place(): pl.pallas_call(place_kernel, out_shape=jax.ShapeDtypeStruct((blocks * BLK...]
    pallas_call x1 -> x0, Pallas kernels: 2.43 us -> none  [prepare(): pl.pallas_call(functools.partial(prepare_kernel, blocks, cap), out_shape=...]
where the time goes in v1:
time: 221 us; the launch traced here: 219 us
  Pallas kernels  219 us (99%)
    pallas_call x1, Pallas kernels, fused(): pl.pallas_call(functools.partial(fused_kernel, kv_heads, cap), out_shape=...  215 us

profile of v1, /device:TPU:21, one launch (start us, length us, event | category | flops | bytes accessed | tf_op | source)
XLA Modules:
  0.0 219.2 jit_solution(2470690653132761686)
XLA Ops:
  0.0 215.2 %fused.1 = (bf16[16,128,2048]{2,1,0:T(8,128)(2,1)S(1)}, s32[16]{0:T(128)S(1)}) custom-call(s32[128]{0:T(128)} %doc_ref.1, s32[128]{0:T(128)} %plan_ref.1, bf16[512,8192]{1,0:T(8,128)(2,1)} %q_ref.1, bf16[512,1024]{1,0:T(8,128)(2,1)} %k_ref.1, bf16[512,1024]{1,0:T(8,128)(2,1)} %v_ref.1), custom_call_target="tpu_custom_call" | custom-call | tf_op jit(solution)/shard_map/fused/pallas_call | solution.py:302
  215.2 4.0 %place.1 = bf16[2048,2048]{1,0:T(8,128)(2,1)} custom-call(s32[16]{0:T(128)S(1)} %get-tuple-element.7.mine_ref, bf16[16,128,2048]{2,1,0:T(8,128)(2,1)S(1)} %get-tuple-element.8.got_ref), custom_call_target="tpu_custom_call" | custom-call | tf_op jit(solution)/shard_map/place/pallas_call | solution.py:354

commit v2 on v1

v2 whole, which is shorter than its diff:
```python
import functools
import math

import jax
import jax.numpy as jnp
from jax import lax
from jax.experimental import pallas as pl
from jax.experimental.pallas import tpu as pltpu
from jax.sharding import PartitionSpec as P

HD = 128
BLK = 128
MAXDOC = 8
HALO = (MAXDOC - 1) * BLK
MESH = pl.DeviceIdType.MESH


def collected_at(n):
    return (n - 1) * 3 // 2


def aligned(x):
    return pl.multiple_of(x, BLK)


def fused_kernel(
    kv_heads,
    cap,
    doc_ref,
    plan_ref,
    q_ref,
    k_ref,
    v_ref,
    got_ref,
    mine_ref,
    slot_block,
    slot_count,
    keys_in,
    values_in,
    stage,
    q_in,
    q_work,
    turned,
    v_work,
    out,
    q_sent,
    q_got,
    kv_sent,
    kv_passed,
    kv_got,
    halo_sent,
    halo_passed,
    halo_got,
    stage_sent,
    stage_got,
    out_sent,
    out_got,
    own_sent,
    own_got,
    ready,
):
    c, h = lax.axis_index("ctx"), lax.axis_index("head")
    nc, nh = lax.axis_size("ctx"), lax.axis_size("head")
    pairs = nh // 2
    pair, side = lax.div(h, 2), lax.rem(h, 2)
    partner = h + 1 - 2 * side
    part = q_ref.shape[0]
    rows = nh * part
    blocks = rows // BLK
    heads = q_in.shape[0]
    shared = 2 * kv_heads
    half = heads // shared
    factor = math.log2(math.e) / math.sqrt(HD)
    sources = (k_ref, v_ref)
    windows = (keys_in, values_in)

    barrier = pltpu.get_barrier_semaphore()
    for d in range(1, nh):
        pl.semaphore_signal(
            barrier, inc=1, device_id=(c, lax.rem(h + d, nh)), device_id_type=MESH
        )

    @pl.when(c > 0)
    def _():
        pl.semaphore_signal(barrier, inc=1, device_id=(c - 1, h), device_id_type=MESH)

    @pl.when(c < nc - 1)
    def _():
        pl.semaphore_signal(barrier, inc=1, device_id=(c + 1, h), device_id_type=MESH)

    near = jnp.where(c > 0, 1, 0) + jnp.where(c < nc - 1, 1, 0)
    pl.semaphore_wait(barrier, nh - 1 + near)

    my_rows = pl.ds(aligned(h * part), part)

    def rows_of(j):
        return pl.ds(aligned(HALO + j * part), part)

    def wait_on(ref, sem):
        pltpu.make_async_copy(ref, ref, sem).wait()

    def send_kv(n):
        for at in range(2):
            dst = windows[at].at[n, rows_of(h)]
            for d in range(pairs):
                other = lax.rem(pair + d, pairs)
                pltpu.make_async_remote_copy(
                    src_ref=sources[at].at[:, pl.ds(aligned((other * shared + n) * HD), HD)],
                    dst_ref=dst,
                    send_sem=kv_sent.at[n, at, d],
                    recv_sem=kv_got.at[n, at, h],
                    device_id=(c, 2 * other + side if d else partner),
                    device_id_type=MESH,
                ).start()
            pltpu.make_async_copy(
                sources[at].at[:, pl.ds(aligned((pair * shared + n) * HD), HD)],
                dst,
                kv_got.at[n, at, h],
            ).start()

    def q_columns(k, t):
        pair_of, side_of = lax.div(t, 2), lax.rem(t, 2)
        n, i = lax.div(k, half), lax.rem(k, half)
        first = 2 * pair_of * heads + n * 2 * half + side_of * half + i
        return pl.ds(aligned(first * HD), HD)

    def send_q(k):
        for d in range(1, nh):
            t = lax.rem(h + d, nh)
            pltpu.make_async_remote_copy(
                src_ref=q_ref.at[:, q_columns(k, t)],
                dst_ref=q_in.at[k, my_rows],
                send_sem=q_sent.at[k, d],
                recv_sem=q_got.at[k, h],
                device_id=(c, t),
                device_id_type=MESH,
            ).start()
        pltpu.make_async_copy(
            q_ref.at[:, q_columns(k, h)], q_in.at[k, my_rows], q_got.at[k, h]
        ).start()

    def send_loop(k, carry):
        send_q(k)
        for n in range(1, shared):

            @pl.when(k == collected_at(n))
            def _(n=n):
                send_kv(n)

        return carry

    send_kv(0)
    lax.fori_loop(0, heads, send_loop, 0)

    step, d = 0, 1
    while d < nc:
        below, above = c >= d, c + d < nc
        for there, other, mark in ((below, c - d, 1), (above, c + d, 0)):

            @pl.when(there)
            def _(other=other, mark=mark, step=step):
                pl.semaphore_signal(
                    ready.at[step, mark], inc=1, device_id=(other, h), device_id_type=MESH
                )

        for there, mark in ((below, 0), (above, 1)):

            @pl.when(there)
            def _(mark=mark, step=step):
                pl.semaphore_wait(ready.at[step, mark], 1)

        step, d = step + 1, 2 * d

    def table(k, carry):
        found = [jnp.int32(0)] * cap
        seen = jnp.int32(0)
        for i in range(blocks):
            p = plan_ref[k * blocks + i]
            hit = lax.div(p, blocks) == c
            for r in range(cap):
                found[r] = jnp.where(hit & (seen == r), lax.rem(p, blocks), found[r])
            seen = seen + jnp.where(hit, 1, 0)
        for r in range(cap):
            at = c * blocks + found[r]
            document = doc_ref[at]
            count = jnp.int32(1)
            for t in range(1, MAXDOC):
                same = doc_ref[jnp.maximum(at - t, 0)] == document
                count = count + jnp.where((at >= t) & same, 1, 0)
            slot_block[k * cap + r] = found[r]
            slot_count[k * cap + r] = count
        return carry

    lax.fori_loop(0, nc, table, 0)

    origins = [lax.div(plan_ref[c * blocks + i], blocks) for i in range(blocks)]
    for i in range(blocks):
        rank = jnp.int32(0)
        for before in range(i):
            rank = rank + jnp.where(origins[before] == origins[i], 1, 0)
        mine_ref[i] = origins[i] * cap + jnp.minimum(rank, cap - 1)

    pieces = []
    for j in range(nh - 1, -1, -1):
        low, high = max(rows - HALO, j * part), (j + 1) * part
        if low < high:
            pieces.append((j, low, high - low))

    odd = lax.rem(c, 2) == 1
    has_next = c < nc - 1

    def for_pieces(mine, act):
        for j, low, size in pieces:

            @pl.when((side == j % 2) if mine else (side != j % 2))
            def _(j=j, low=low, size=size):
                act(j, low, size)

    def halo_copy(n, at, j, low, size):
        ref = windows[at]
        return pltpu.make_async_remote_copy(
            src_ref=ref.at[n, pl.ds(HALO + low, size)],
            dst_ref=ref.at[n, pl.ds(HALO + low - rows, size)],
            send_sem=halo_sent.at[n, at, j],
            recv_sem=halo_got.at[n, at, j],
            device_id=(jnp.minimum(c + 1, nc - 1), h),
            device_id_type=MESH,
        )

    def detour_copy(n, j, low, size):
        return pltpu.make_async_remote_copy(
            src_ref=values_in.at[n, pl.ds(HALO + low, size)],
            dst_ref=stage.at[n, pl.ds(HALO + low - rows, size)],
            send_sem=halo_sent.at[n, 1, j],
            recv_sem=stage_got.at[n, j],
            device_id=(jnp.maximum(c - 1, 0), h),
            device_id_type=MESH,
        )

    def relay_copy(n, j, low, size):
        held = pl.ds(HALO + low - rows, size)
        return pltpu.make_async_remote_copy(
            src_ref=stage.at[n, held],
            dst_ref=values_in.at[n, held],
            send_sem=stage_sent.at[n, j],
            recv_sem=halo_got.at[n, 1, j],
            device_id=(jnp.minimum(c + 2, nc - 1), h),
            device_id_type=MESH,
        )

    def pass_halo_copy(n, at, j, low, size):
        ref = windows[at].at[n, pl.ds(HALO + low - rows, size)]
        return pltpu.make_async_remote_copy(
            src_ref=ref,
            dst_ref=ref,
            send_sem=halo_passed.at[n, at, j],
            recv_sem=halo_got.at[n, at, j],
            device_id=(c, partner),
            device_id_type=MESH,
        )

    def pass_kv_copy(n, at, d):
        j = 2 * lax.rem(pair + d, pairs) + side
        ref = windows[at].at[n, rows_of(j)]
        return pltpu.make_async_remote_copy(
            src_ref=ref,
            dst_ref=ref,
            send_sem=kv_passed.at[n, at, d],
            recv_sem=kv_got.at[n, at, j],
            device_id=(c, partner),
            device_id_type=MESH,
        )

    def collect(n):
        for at in range(2):
            for d in range(pairs):
                j = 2 * lax.rem(pair + d, pairs) + side
                wait_on(windows[at].at[n, rows_of(j)], kv_got.at[n, at, j])
                if d:
                    pass_kv_copy(n, at, d).start()

            straight = has_next
            if at and n:
                straight = has_next & jnp.logical_not(odd)

                @pl.when(has_next & odd)
                def _():
                    for_pieces(True, lambda *p: detour_copy(n, *p).start())

            @pl.when(straight)
            def _(at=at):
                for_pieces(True, lambda *p: halo_copy(n, at, *p).start())

    relays = jnp.logical_not(odd) & (c + 2 < nc)

    def relay(n):
        @pl.when(relays)
        def _():
            def act(*p):
                relay_copy(n, *p).start()

            def arrived(j, low, size):
                wait_on(stage.at[n, pl.ds(HALO + low - rows, size)], stage_got.at[n, j])
                act(j, low, size)

            for_pieces(True, arrived)

    def pass_halo(n):
        @pl.when(c > 0)
        def _():
            for at in range(2):

                def act(j, low, size, at=at):
                    held = windows[at].at[n, pl.ds(HALO + low - rows, size)]
                    wait_on(held, halo_got.at[n, at, j])
                    pass_halo_copy(n, at, j, low, size).start()

                for_pieces(True, act)

    def turn(n, first, last):
        for i in range(first, last):
            turned[i] = keys_in[n, i * BLK : (i + 1) * BLK, :].T
            v_work[i] = values_in[n, i * BLK : (i + 1) * BLK, :]

    def turn_rows(n):
        for at in range(2):
            for other in range(pairs):
                j = 2 * other + 1 - side
                wait_on(windows[at].at[n, rows_of(j)], kv_got.at[n, at, j])
        turn(n, MAXDOC - 1, MAXDOC - 1 + blocks)

    def turn_halo(n):
        @pl.when(c > 0)
        def _():
            for at in range(2):

                def act(j, low, size, at=at):
                    held = windows[at].at[n, pl.ds(HALO + low - rows, size)]
                    wait_on(held, halo_got.at[n, at, j])

                for_pieces(False, act)
            turn(n, 0, MAXDOC - 1)

        @pl.when(c == 0)
        def _():
            for ref in (turned, v_work):
                ref[0 : MAXDOC - 1] = jnp.zeros((MAXDOC - 1,) + ref.shape[1:], ref.dtype)

    causal = lax.broadcasted_iota(jnp.int32, (BLK, BLK), 1) <= lax.broadcasted_iota(
        jnp.int32, (BLK, BLK), 0
    )

    def attend(k, slot):
        block = slot_block[slot]
        count = slot_count[slot]
        queries = q_work[block]
        keys = jnp.concatenate([turned[block + i] for i in range(MAXDOC)], axis=1)
        values = jnp.concatenate([v_work[block + i] for i in range(MAXDOC)], axis=0)
        scores = jnp.dot(queries, keys, preferred_element_type=jnp.float32)
        parts = [scores[:, i * BLK : (i + 1) * BLK] for i in range(MAXDOC)]
        for i in range(MAXDOC - 1):
            inside = jnp.full((BLK, BLK), count - (MAXDOC - 1 - i), jnp.int32) > 0
            parts[i] = jnp.where(inside, parts[i], -jnp.inf)
        parts[-1] = jnp.where(causal, parts[-1], -jnp.inf)
        top = jnp.max(functools.reduce(jnp.maximum, parts), axis=1, keepdims=True)
        parts = [jnp.exp2((x - top) * factor) for x in parts]
        total = jnp.sum(functools.reduce(jnp.add, parts), axis=1, keepdims=True)
        weights = jnp.concatenate([x.astype(jnp.bfloat16) for x in parts], axis=1)
        mixed = jnp.dot(weights, values, preferred_element_type=jnp.float32) / total
        out[k, slot] = mixed.astype(out.dtype)

    def owner(k):
        return 2 * pair + lax.div(lax.div(k, half), kv_heads)

    def column(k):
        n, i = lax.div(k, half), lax.rem(k, half)
        return lax.rem(n, kv_heads) * 2 * half + side * half + i

    def columns(col):
        return pl.ds(aligned(col * HD), HD)

    def send_out(k, d):
        t = lax.rem(c + d, nc)
        col = column(k)
        pltpu.make_async_remote_copy(
            src_ref=out.at[k, pl.ds(t * cap, cap)],
            dst_ref=got_ref.at[pl.ds(c * cap, cap), :, columns(col)],
            send_sem=out_sent.at[k],
            recv_sem=out_got.at[col],
            device_id=(t, owner(k)),
            device_id_type=MESH,
        ).start()

    own_slots = pl.ds(c * cap, cap)

    def send_own(k):
        col = column(k)
        src = out.at[k, own_slots]
        dst = got_ref.at[own_slots, :, columns(col)]

        @pl.when(owner(k) == h)
        def _():
            pltpu.make_async_copy(src, dst, own_got.at[col]).start()

        @pl.when(owner(k) != h)
        def _():
            pltpu.make_async_remote_copy(
                src_ref=src,
                dst_ref=dst,
                send_sem=own_sent.at[k],
                recv_sem=own_got.at[col],
                device_id=(c, partner),
                device_id_type=MESH,
            ).start()

    def head_step(k):
        for j in range(nh):
            wait_on(q_in.at[k, pl.ds(j * part, part)], q_got.at[k, j])
        q_work[...] = q_in[k].reshape(q_work.shape)

        def target(d, carry):
            t = lax.rem(c + d, nc)
            for r in range(cap):
                attend(k, t * cap + r)
                if r == 0:

                    @pl.when(d > 1)
                    def _():
                        send_out(k, d - 1)

            return carry

        lax.fori_loop(1, nc + 1, target, 0)
        send_own(k)

    collect(0)
    turn_rows(0)
    pass_halo(0)
    turn_halo(0)

    def one(k, carry):
        n, i = lax.div(k, half), lax.rem(k, half)

        @pl.when((i == 0) & (n > 0))
        def _():
            turn_rows(n)
            turn_halo(n)

        head_step(k)
        for later in range(1, shared):
            for wait, act in ((2, pass_halo), (1, relay), (0, collect)):

                @pl.when(k == collected_at(later) + wait)
                def _(later=later, act=act):
                    act(later)

        return carry

    lax.fori_loop(0, heads, one, 0)

    def settle_kv(n, first):
        for at in range(2):
            for d in range(pairs):
                wait_on(windows[at].at[n, rows_of(h)], kv_sent.at[n, at, d])
                if d:
                    pass_kv_copy(n, at, d).wait_send()

            @pl.when(has_next)
            def _(at=at):
                for_pieces(True, lambda *p: halo_copy(n, at, *p).wait_send())

            @pl.when(c > 0)
            def _(at=at):
                for_pieces(True, lambda *p: pass_halo_copy(n, at, *p).wait_send())

        if not first:

            @pl.when(relays)
            def _():
                for_pieces(True, lambda *p: relay_copy(n, *p).wait_send())

    settle_kv(0, True)

    def settle(n, carry):
        settle_kv(n, False)
        return carry

    lax.fori_loop(1, shared, settle, 0)

    def drain(k, carry):
        for d in range(1, nh):
            wait_on(q_in.at[k, my_rows], q_sent.at[k, d])

        @pl.when(owner(k) != h)
        def _():
            wait_on(out.at[k, own_slots], own_sent.at[k])

        wait_on(out.at[k, pl.ds(0, (nc - 1) * cap)], out_sent.at[k])
        wait_on(got_ref.at[own_slots, :, columns(k)], own_got.at[k])
        wait_on(got_ref.at[pl.ds(0, (nc - 1) * cap), :, columns(k)], out_got.at[k])
        return carry

    lax.fori_loop(0, heads, drain, 0)


def fused(doc_ids, plan, query, key, value):
    nc, nh = lax.axis_size("ctx"), lax.axis_size("head")
    part = query.shape[0]
    rows = nh * part
    blocks = rows // BLK
    heads = query.shape[1] // nh // HD
    kv_heads = key.shape[1] // nh // HD
    shared = 2 * kv_heads
    cap = -(-blocks // nc)
    slots = nc * cap
    window = HALO + rows
    dma = pltpu.SemaphoreType.DMA
    buffers = [
        (shared, window, HD),
        (shared, window, HD),
        (shared, HALO, HD),
        (heads, rows, HD),
        (blocks, BLK, HD),
        (window // BLK, HD, BLK),
        (window // BLK, BLK, HD),
        (heads, slots, BLK, HD),
    ]
    held = 2 * sum(math.prod(shape) for shape in buffers)
    return pl.pallas_call(
        functools.partial(fused_kernel, kv_heads, cap),
        out_shape=[
            jax.ShapeDtypeStruct((slots, BLK, heads * HD), query.dtype),
            jax.ShapeDtypeStruct((blocks,), jnp.int32),
        ],
        in_specs=[pl.BlockSpec(memory_space=pltpu.SMEM)] * 2
        + [pl.BlockSpec(memory_space=pltpu.HBM)] * 3,
        out_specs=[
            pl.BlockSpec(memory_space=pl.ANY),
            pl.BlockSpec(memory_space=pltpu.SMEM),
        ],
        scratch_shapes=[pltpu.SMEM((slots,), jnp.int32)] * 2
        + [pltpu.VMEM(shape, query.dtype) for shape in buffers]
        + [dma((heads, nh))] * 2
        + [dma((shared, 2, nh))] * 6
        + [dma((shared, nh))] * 2
        + [dma((heads,))] * 4
        + [pltpu.SemaphoreType.REGULAR((nc.bit_length(), 2))],
        compiler_params=pltpu.CompilerParams(
            collective_id=0, has_side_effects=True, vmem_limit_bytes=held + (6 << 20)
        ),
        name="fused",
    )(doc_ids, plan, query, key, value)


def place_kernel(mine_ref, got_ref, o_ref, sems):
    copies = []
    for i in range(o_ref.shape[0] // BLK):
        copy = pltpu.make_async_copy(
            got_ref.at[mine_ref[i]], o_ref.at[pl.ds(i * BLK, BLK)], sems.at[i]
        )
        copy.start()
        copies.append(copy)
    for copy in copies:
        copy.wait()


def place(mine, got):
    blocks = mine.shape[0]
    width = got.shape[2]
    return pl.pallas_call(
        place_kernel,
        out_shape=jax.ShapeDtypeStruct((blocks * BLK, width), got.dtype),
        in_specs=[
            pl.BlockSpec(memory_space=pltpu.SMEM),
            pl.BlockSpec(memory_space=pl.ANY),
        ],
        out_specs=pl.BlockSpec(memory_space=pl.ANY),
        scratch_shapes=[pltpu.SemaphoreType.DMA((blocks,))],
        compiler_params=pltpu.CompilerParams(vmem_limit_bytes=1 << 20),
        name="place",
    )(mine, got)


def shards(query, key, value, doc_ids, plan):
    operands = [
        pltpu.with_memory_space_constraint(x, pltpu.HBM)
        for x in (doc_ids, plan, query, key, value)
    ]
    got, mine = fused(*operands)
    return place(mine, got)


def solution(mesh):
    return jax.shard_map(
        shards,
        mesh=mesh,
        in_specs=(
            P(("ctx", "head"), None),
            P(("ctx", "head"), None),
            P(("ctx", "head"), None),
            P(),
            P(),
        ),
        out_specs=P("ctx", "head"),
        check_vma=False,
    )
```

time: 221 us -> 217 us (0.982)
  Pallas kernels: 219 us -> 214 us
    pallas_call x1, Pallas kernels: 215 us -> 210 us  [fused(): pl.pallas_call(functools.partial(fused_kernel, kv_heads, cap), out_shape=...]
where the time goes in v2:
time: 217 us; the launch traced here: 214 us
  Pallas kernels  214 us (99%)
    pallas_call x1, Pallas kernels, fused(): pl.pallas_call(functools.partial(fused_kernel, kv_heads, cap), out_shape=...  210 us

profile of v2, /device:TPU:21, one launch (start us, length us, event | category | flops | bytes accessed | tf_op | source)
XLA Modules:
  0.0 214.0 jit_solution(4732572849116796152)
XLA Ops:
  0.0 210.1 %fused.1 = (bf16[16,128,2048]{2,1,0:T(8,128)(2,1)S(1)}, s32[16]{0:T(128)S(1)}) custom-call(s32[128]{0:T(128)} %doc_ref.1, s32[128]{0:T(128)} %plan_ref.1, bf16[512,8192]{1,0:T(8,128)(2,1)} %q_ref.1, bf16[512,1024]{1,0:T(8,128)(2,1)} %k_ref.1, bf16[512,1024]{1,0:T(8,128)(2,1)} %v_ref.1), custom_call_target="tpu_custom_call" | custom-call | tf_op jit(solution)/shard_map/fused/pallas_call | solution.py:529
  210.1 4.0 %place.1 = bf16[2048,2048]{1,0:T(8,128)(2,1)} custom-call(s32[16]{0:T(128)S(1)} %get-tuple-element.7.mine_ref, bf16[16,128,2048]{2,1,0:T(8,128)(2,1)S(1)} %get-tuple-element.8.got_ref), custom_call_target="tpu_custom_call" | custom-call | tf_op jit(solution)/shard_map/place/pallas_call | solution.py:570

commit v3 on v2

--- a/solution.py
+++ b/solution.py
@@ -379,8 +379,12 @@
     def columns(col):
         return pl.ds(aligned(col * HD), HD)
 
-    def send_out(k, d):
-        t = lax.rem(c + d, nc)
+    def target_of(s):
+        away = nc // 2 + (1 - 2 * lax.rem(s, 2)) * lax.div(s + 1, 2)
+        return lax.rem(c + away, nc)
+
+    def send_out(k, s):
+        t = target_of(s)
         col = column(k)
         pltpu.make_async_remote_copy(
             src_ref=out.at[k, pl.ds(t * cap, cap)],
@@ -418,19 +422,19 @@
             wait_on(q_in.at[k, pl.ds(j * part, part)], q_got.at[k, j])
         q_work[...] = q_in[k].reshape(q_work.shape)
 
-        def target(d, carry):
-            t = lax.rem(c + d, nc)
+        def target(s, carry):
+            t = target_of(s)
             for r in range(cap):
                 attend(k, t * cap + r)
                 if r == 0:
 
-                    @pl.when(d > 1)
+                    @pl.when(s > 0)
                     def _():
-                        send_out(k, d - 1)
+                        send_out(k, s - 1)
 
             return carry
 
-        lax.fori_loop(1, nc + 1, target, 0)
+        lax.fori_loop(0, nc, target, 0)
         send_own(k)
 
     collect(0)

time: 217 us -> 215 us (level); the launches traced: 214 us -> 214 us
  no operation moved by 1% of the time
where the time goes in v3:
time: 215 us; the launch traced here: 214 us
  Pallas kernels  214 us (100%)
    pallas_call x1, Pallas kernels, fused(): pl.pallas_call(functools.partial(fused_kernel, kv_heads, cap), out_shape=...  210 us

profile of v3, /device:TPU:21, one launch (start us, length us, event | category | flops | bytes accessed | tf_op | source)
XLA Modules:
  0.0 214.3 jit_solution(12744627764593713624)
XLA Ops:
  0.0 210.3 %fused.1 = (bf16[16,128,2048]{2,1,0:T(8,128)(2,1)S(1)}, s32[16]{0:T(128)S(1)}) custom-call(s32[128]{0:T(128)} %doc_ref.1, s32[128]{0:T(128)} %plan_ref.1, bf16[512,8192]{1,0:T(8,128)(2,1)} %q_ref.1, bf16[512,1024]{1,0:T(8,128)(2,1)} %k_ref.1, bf16[512,1024]{1,0:T(8,128)(2,1)} %v_ref.1), custom_call_target="tpu_custom_call" | custom-call | tf_op jit(solution)/shard_map/fused/pallas_call | solution.py:533
  210.3 4.0 %place.1 = bf16[2048,2048]{1,0:T(8,128)(2,1)} custom-call(s32[16]{0:T(128)S(1)} %get-tuple-element.7.mine_ref, bf16[16,128,2048]{2,1,0:T(8,128)(2,1)S(1)} %get-tuple-element.8.got_ref), custom_call_target="tpu_custom_call" | custom-call | tf_op jit(solution)/shard_map/place/pallas_call | solution.py:574

commit v4 on v3

--- a/solution.py
+++ b/solution.py
@@ -12,11 +12,9 @@
 BLK = 128
 MAXDOC = 8
 HALO = (MAXDOC - 1) * BLK
+AHEAD = 8
+DIRECT = 3
 MESH = pl.DeviceIdType.MESH
-
-
-def collected_at(n):
-    return (n - 1) * 3 // 2
 
 
 def aligned(x):
@@ -37,6 +35,7 @@
     slot_count,
     keys_in,
     values_in,
+    via,
     stage,
     q_in,
     q_work,
@@ -51,8 +50,11 @@
     halo_sent,
     halo_passed,
     halo_got,
+    away_sent,
+    via_got,
+    via_sent,
+    stage_got,
     stage_sent,
-    stage_got,
     out_sent,
     out_got,
     own_sent,
@@ -139,18 +141,104 @@
             q_ref.at[:, q_columns(k, h)], q_in.at[k, my_rows], q_got.at[k, h]
         ).start()
 
-    def send_loop(k, carry):
+    pieces = []
+    for j in range(nh - 1, -1, -1):
+        low, high = max(rows - HALO, j * part), (j + 1) * part
+        if low < high:
+            pieces.append((j, low, high - low))
+
+    odd = lax.rem(c, 2) == 1
+    has_next = c < nc - 1
+    following = jnp.minimum(c + 1, nc - 1)
+    relays = jnp.logical_not(odd) & (c + 2 < nc)
+
+    def for_pieces(mine, act):
+        for j, low, size in pieces:
+
+            @pl.when((side == j % 2) if mine else (side != j % 2))
+            def _(j=j, low=low, size=size):
+                act(j, low, size)
+
+    def for_own_pieces(act):
+        for j, low, size in pieces:
+
+            @pl.when(h == j)
+            def _(j=j, low=low, size=size):
+                act(j, low, size)
+
+    def for_other_pairs(act):
+        for at in range(2):
+            for d in range(1, pairs):
+                act(at, d)
+
+    def halo_rows(low, size):
+        return pl.ds(HALO + low - rows, size)
+
+    def rows_in(at, n, d, j, low, size):
+        other = lax.rem(pair + d, pairs)
+        return sources[at].at[
+            pl.ds(low - j * part, size), pl.ds(aligned((other * shared + n) * HD), HD)
+        ]
+
+    def halo_copy(n, at, j, low, size, src):
+        return pltpu.make_async_remote_copy(
+            src_ref=src,
+            dst_ref=windows[at].at[n, halo_rows(low, size)],
+            send_sem=halo_sent.at[n, at, j],
+            recv_sem=halo_got.at[n, at, j],
+            device_id=(following, h),
+            device_id_type=MESH,
+        )
+
+    def place_of(n, d):
+        return (d - 1) * (shared - DIRECT) + n - DIRECT
+
+    def away_copy(n, at, d, j, low, size, back):
+        q = place_of(n, d)
+        return pltpu.make_async_remote_copy(
+            src_ref=rows_in(at, n, d, j, low, size),
+            dst_ref=(via if back else stage).at[at, q, halo_rows(low, size)],
+            send_sem=away_sent.at[at, q, j],
+            recv_sem=(via_got if back else stage_got).at[at, q, j],
+            device_id=(jnp.maximum(c - 1, 0) if back else following, h),
+            device_id_type=MESH,
+        )
+
+    def lead(n, who):
+        @pl.when(has_next & who)
+        def _():
+            def own_pair(j, low, size):
+                for at in range(2):
+                    src = rows_in(at, n, 0, j, low, size)
+                    halo_copy(n, at, j, low, size, src).start()
+
+            for_own_pieces(own_pair)
+
+        if n >= DIRECT:
+            for back, turn_of in ((True, odd), (False, jnp.logical_not(odd))):
+
+                @pl.when(has_next & who & turn_of)
+                def _(back=back):
+                    for_own_pieces(
+                        lambda *p: for_other_pairs(
+                            lambda at, d: away_copy(n, at, d, *p, back).start()
+                        )
+                    )
+
+    def send_kv_after(k):
+        for n in range(1, shared):
+            if k == 2 * n - 2:
+                send_kv(n)
+
+    always = c >= 0
+    lead(0, always)
+    send_kv(0)
+    for k in range(min(AHEAD, heads)):
         send_q(k)
-        for n in range(1, shared):
-
-            @pl.when(k == collected_at(n))
-            def _(n=n):
-                send_kv(n)
-
-        return carry
-
-    send_kv(0)
-    lax.fori_loop(0, heads, send_loop, 0)
+        send_kv_after(k)
+        if k == 0:
+            for n in range(1, shared):
+                lead(n, always if n == 1 else odd)
 
     step, d = 0, 1
     while d < nc:
@@ -200,56 +288,8 @@
             rank = rank + jnp.where(origins[before] == origins[i], 1, 0)
         mine_ref[i] = origins[i] * cap + jnp.minimum(rank, cap - 1)
 
-    pieces = []
-    for j in range(nh - 1, -1, -1):
-        low, high = max(rows - HALO, j * part), (j + 1) * part
-        if low < high:
-            pieces.append((j, low, high - low))
-
-    odd = lax.rem(c, 2) == 1
-    has_next = c < nc - 1
-
-    def for_pieces(mine, act):
-        for j, low, size in pieces:
-
-            @pl.when((side == j % 2) if mine else (side != j % 2))
-            def _(j=j, low=low, size=size):
-                act(j, low, size)
-
-    def halo_copy(n, at, j, low, size):
-        ref = windows[at]
-        return pltpu.make_async_remote_copy(
-            src_ref=ref.at[n, pl.ds(HALO + low, size)],
-            dst_ref=ref.at[n, pl.ds(HALO + low - rows, size)],
-            send_sem=halo_sent.at[n, at, j],
-            recv_sem=halo_got.at[n, at, j],
-            device_id=(jnp.minimum(c + 1, nc - 1), h),
-            device_id_type=MESH,
-        )
-
-    def detour_copy(n, j, low, size):
-        return pltpu.make_async_remote_copy(
-            src_ref=values_in.at[n, pl.ds(HALO + low, size)],
-            dst_ref=stage.at[n, pl.ds(HALO + low - rows, size)],
-            send_sem=halo_sent.at[n, 1, j],
-            recv_sem=stage_got.at[n, j],
-            device_id=(jnp.maximum(c - 1, 0), h),
-            device_id_type=MESH,
-        )
-
-    def relay_copy(n, j, low, size):
-        held = pl.ds(HALO + low - rows, size)
-        return pltpu.make_async_remote_copy(
-            src_ref=stage.at[n, held],
-            dst_ref=values_in.at[n, held],
-            send_sem=stage_sent.at[n, j],
-            recv_sem=halo_got.at[n, 1, j],
-            device_id=(jnp.minimum(c + 2, nc - 1), h),
-            device_id_type=MESH,
-        )
-
     def pass_halo_copy(n, at, j, low, size):
-        ref = windows[at].at[n, pl.ds(HALO + low - rows, size)]
+        ref = windows[at].at[n, halo_rows(low, size)]
         return pltpu.make_async_remote_copy(
             src_ref=ref,
             dst_ref=ref,
@@ -278,32 +318,104 @@
                 wait_on(windows[at].at[n, rows_of(j)], kv_got.at[n, at, j])
                 if d:
                     pass_kv_copy(n, at, d).start()
-
-            straight = has_next
-            if at and n:
-                straight = has_next & jnp.logical_not(odd)
-
-                @pl.when(has_next & odd)
+            if n >= DIRECT:
+                continue
+
+            def act(j, low, size, at=at):
+                @pl.when((h != j) & (odd if n and at else False))
                 def _():
-                    for_pieces(True, lambda *p: detour_copy(n, *p).start())
-
-            @pl.when(straight)
-            def _(at=at):
-                for_pieces(True, lambda *p: halo_copy(n, at, *p).start())
-
-    relays = jnp.logical_not(odd) & (c + 2 < nc)
+                    detour_copy(n, j, low, size).start()
+
+                @pl.when((h != j) & jnp.logical_not(odd if n and at else False))
+                def _():
+                    src = windows[at].at[n, pl.ds(HALO + low, size)]
+                    halo_copy(n, at, j, low, size, src).start()
+
+            @pl.when(has_next)
+            def _(act=act):
+                for_pieces(True, act)
+
+    def detour_copy(n, j, low, size):
+        return pltpu.make_async_remote_copy(
+            src_ref=values_in.at[n, pl.ds(HALO + low, size)],
+            dst_ref=via.at[1, n - 1, halo_rows(low, size)],
+            send_sem=halo_sent.at[n, 1, j],
+            recv_sem=via_got.at[1, n - 1, j],
+            device_id=(jnp.maximum(c - 1, 0), h),
+            device_id_type=MESH,
+        )
+
+    def detour_on_copy(n, j, low, size):
+        held = halo_rows(low, size)
+        return pltpu.make_async_remote_copy(
+            src_ref=via.at[1, n - 1, held],
+            dst_ref=values_in.at[n, held],
+            send_sem=via_sent.at[1, n - 1, j],
+            recv_sem=halo_got.at[n, 1, j],
+            device_id=(jnp.minimum(c + 2, nc - 1), h),
+            device_id_type=MESH,
+        )
+
+    def detour_on(n):
+        @pl.when(relays)
+        def _():
+            def act(j, low, size):
+                @pl.when(h != j)
+                def _():
+                    wait_on(via.at[1, n - 1, halo_rows(low, size)], via_got.at[1, n - 1, j])
+                    detour_on_copy(n, j, low, size).start()
+
+            for_pieces(True, act)
+
+    def relay_copy(n, at, d, j, low, size):
+        q = place_of(n, d)
+        held = halo_rows(low, size)
+        return pltpu.make_async_remote_copy(
+            src_ref=via.at[at, q, held],
+            dst_ref=stage.at[at, q, held],
+            send_sem=via_sent.at[at, q, j],
+            recv_sem=stage_got.at[at, q, j],
+            device_id=(jnp.minimum(c + 2, nc - 1), h),
+            device_id_type=MESH,
+        )
 
     def relay(n):
         @pl.when(relays)
         def _():
-            def act(*p):
-                relay_copy(n, *p).start()
-
-            def arrived(j, low, size):
-                wait_on(stage.at[n, pl.ds(HALO + low - rows, size)], stage_got.at[n, j])
-                act(j, low, size)
-
-            for_pieces(True, arrived)
+            def act(j, low, size):
+                def one_of(at, d):
+                    q = place_of(n, d)
+                    wait_on(via.at[at, q, halo_rows(low, size)], via_got.at[at, q, j])
+                    relay_copy(n, at, d, j, low, size).start()
+
+                for_other_pairs(one_of)
+
+            for_own_pieces(act)
+
+    def spread_copy(n, at, d, j, low, size):
+        q = place_of(n, d)
+        held = halo_rows(low, size)
+        return pltpu.make_async_remote_copy(
+            src_ref=stage.at[at, q, held],
+            dst_ref=windows[at].at[n, held],
+            send_sem=stage_sent.at[at, q, j],
+            recv_sem=halo_got.at[n, at, j],
+            device_id=(c, 2 * lax.rem(pair + d, pairs) + side),
+            device_id_type=MESH,
+        )
+
+    def spread(n):
+        @pl.when(c > 0)
+        def _():
+            def act(j, low, size):
+                def one_of(at, d):
+                    q = place_of(n, d)
+                    wait_on(stage.at[at, q, halo_rows(low, size)], stage_got.at[at, q, j])
+                    spread_copy(n, at, d, j, low, size).start()
+
+                for_other_pairs(one_of)
+
+            for_own_pieces(act)
 
     def pass_halo(n):
         @pl.when(c > 0)
@@ -311,7 +423,7 @@
             for at in range(2):
 
                 def act(j, low, size, at=at):
-                    held = windows[at].at[n, pl.ds(HALO + low - rows, size)]
+                    held = windows[at].at[n, halo_rows(low, size)]
                     wait_on(held, halo_got.at[n, at, j])
                     pass_halo_copy(n, at, j, low, size).start()
 
@@ -335,7 +447,7 @@
             for at in range(2):
 
                 def act(j, low, size, at=at):
-                    held = windows[at].at[n, pl.ds(HALO + low - rows, size)]
+                    held = windows[at].at[n, halo_rows(low, size)]
                     wait_on(held, halo_got.at[n, at, j])
 
                 for_pieces(False, act)
@@ -451,45 +563,88 @@
             turn_halo(n)
 
         head_step(k)
+        def after(head, act):
+            pl.when(k == head)(act)
+
+        for later in range(2, shared):
+            after(later - 2, functools.partial(lead, later, jnp.logical_not(odd)))
+        for later in range(DIRECT, shared):
+            after(later - DIRECT, functools.partial(relay, later))
+            after(later, functools.partial(spread, later))
+
+        @pl.when(k + AHEAD < heads)
+        def _():
+            send_q(k + AHEAD)
+
+        for later in range(1, min(DIRECT, shared)):
+            after(2 * later - 1, functools.partial(detour_on, later))
         for later in range(1, shared):
-            for wait, act in ((2, pass_halo), (1, relay), (0, collect)):
-
-                @pl.when(k == collected_at(later) + wait)
-                def _(later=later, act=act):
-                    act(later)
-
+            after(2 * later - 2, functools.partial(collect, later))
+            last = later * half - 1
+            after(last - 1 if later == 1 else last, functools.partial(pass_halo, later))
         return carry
 
     lax.fori_loop(0, heads, one, 0)
 
-    def settle_kv(n, first):
+    def settle_kv(n):
         for at in range(2):
             for d in range(pairs):
                 wait_on(windows[at].at[n, rows_of(h)], kv_sent.at[n, at, d])
                 if d:
                     pass_kv_copy(n, at, d).wait_send()
 
-            @pl.when(has_next)
-            def _(at=at):
-                for_pieces(True, lambda *p: halo_copy(n, at, *p).wait_send())
-
             @pl.when(c > 0)
             def _(at=at):
                 for_pieces(True, lambda *p: pass_halo_copy(n, at, *p).wait_send())
 
-        if not first:
+            def sent(j, low, size, at=at):
+                wait_on(windows[at].at[n, halo_rows(low, size)], halo_sent.at[n, at, j])
+
+            @pl.when(has_next)
+            def _(sent=sent):
+                if n >= DIRECT:
+                    for_own_pieces(sent)
+                else:
+                    for_pieces(True, sent)
+
+        if 0 < n < DIRECT:
 
             @pl.when(relays)
             def _():
-                for_pieces(True, lambda *p: relay_copy(n, *p).wait_send())
-
-    settle_kv(0, True)
-
-    def settle(n, carry):
-        settle_kv(n, False)
-        return carry
-
-    lax.fori_loop(1, shared, settle, 0)
+                def sent_on(j, low, size):
+                    @pl.when(h != j)
+                    def _():
+                        wait_on(
+                            via.at[1, n - 1, halo_rows(low, size)], via_sent.at[1, n - 1, j]
+                        )
+
+                for_pieces(True, sent_on)
+
+        if n >= DIRECT:
+
+            def for_places(act):
+                for_own_pieces(
+                    lambda *p: for_other_pairs(lambda at, d: act(at, place_of(n, d), *p))
+                )
+
+            def settled(buffer, sems):
+                def act(at, q, j, low, size):
+                    wait_on(buffer.at[at, q, halo_rows(low, size)], sems.at[at, q, j])
+
+                return act
+
+            for cond, buffer, sems in (
+                (has_next, stage, away_sent),
+                (relays, via, via_sent),
+                (c > 0, stage, stage_sent),
+            ):
+
+                @pl.when(cond)
+                def _(buffer=buffer, sems=sems):
+                    for_places(settled(buffer, sems))
+
+    for n in range(shared):
+        settle_kv(n)
 
     def drain(k, carry):
         for d in range(1, nh):
@@ -515,6 +670,7 @@
     heads = query.shape[1] // nh // HD
     kv_heads = key.shape[1] // nh // HD
     shared = 2 * kv_heads
+    places = max(DIRECT - 1, (nh // 2 - 1) * (shared - DIRECT))
     cap = -(-blocks // nc)
     slots = nc * cap
     window = HALO + rows
@@ -522,7 +678,8 @@
     buffers = [
         (shared, window, HD),
         (shared, window, HD),
-        (shared, HALO, HD),
+        (2, places, HALO, HD),
+        (2, places, HALO, HD),
         (heads, rows, HD),
         (blocks, BLK, HD),
         (window // BLK, HD, BLK),
@@ -546,7 +703,7 @@
         + [pltpu.VMEM(shape, query.dtype) for shape in buffers]
         + [dma((heads, nh))] * 2
         + [dma((shared, 2, nh))] * 6
-        + [dma((shared, nh))] * 2
+        + [dma((2, places, nh))] * 5
         + [dma((heads,))] * 4
         + [pltpu.SemaphoreType.REGULAR((nc.bit_length(), 2))],
         compiler_params=pltpu.CompilerParams(

time: 215 us -> 213 us (level)
  no operation moved by 1% of the time
where the time goes in v4:
time: 213 us
  Pallas kernels  213 us (100%)
    pallas_call x1, Pallas kernels, fused(): pl.pallas_call(functools.partial(fused_kernel, kv_heads, cap), out_shape=...  209 us

profile of v4, /device:TPU:21, one launch (start us, length us, event | category | flops | bytes accessed | tf_op | source)
XLA Modules:
  0.0 212.9 jit_solution(10933753229998015892)
XLA Ops:
  0.0 208.9 %fused.1 = (bf16[16,128,2048]{2,1,0:T(8,128)(2,1)S(1)}, s32[16]{0:T(128)S(1)}) custom-call(s32[128]{0:T(128)} %doc_ref.1, s32[128]{0:T(128)} %plan_ref.1, bf16[512,8192]{1,0:T(8,128)(2,1)} %q_ref.1, bf16[512,1024]{1,0:T(8,128)(2,1)} %k_ref.1, bf16[512,1024]{1,0:T(8,128)(2,1)} %v_ref.1), custom_call_target="tpu_custom_call" | custom-call | tf_op jit(solution)/shard_map/fused/pallas_call | solution.py:690
  208.9 4.0 %place.1 = bf16[2048,2048]{1,0:T(8,128)(2,1)} custom-call(s32[16]{0:T(128)S(1)} %get-tuple-element.7.mine_ref, bf16[16,128,2048]{2,1,0:T(8,128)(2,1)S(1)} %get-tuple-element.8.got_ref), custom_call_target="tpu_custom_call" | custom-call | tf_op jit(solution)/shard_map/place/pallas_call | solution.py:731

commit v5 on v4

--- a/solution.py
+++ b/solution.py
@@ -24,12 +24,15 @@
 def fused_kernel(
     kv_heads,
     cap,
-    doc_ref,
-    plan_ref,
+    doc_hbm,
+    plan_hbm,
     q_ref,
     k_ref,
     v_ref,
     got_ref,
+    mine_out,
+    doc_ref,
+    plan_ref,
     mine_ref,
     slot_block,
     slot_count,
@@ -59,6 +62,7 @@
     out_got,
     own_sent,
     own_got,
+    index_sems,
     ready,
 ):
     c, h = lax.axis_index("ctx"), lax.axis_index("head")
@@ -90,6 +94,13 @@
     def _():
         pl.semaphore_signal(barrier, inc=1, device_id=(c + 1, h), device_id_type=MESH)
 
+    index_copies = [
+        pltpu.make_async_copy(doc_hbm, doc_ref, index_sems.at[0]),
+        pltpu.make_async_copy(plan_hbm, plan_ref, index_sems.at[1]),
+    ]
+    mine_copy = pltpu.make_async_copy(mine_ref, mine_out, index_sems.at[2])
+    for copy in index_copies:
+        copy.start()
     near = jnp.where(c > 0, 1, 0) + jnp.where(c < nc - 1, 1, 0)
     pl.semaphore_wait(barrier, nh - 1 + near)
 
@@ -258,6 +269,9 @@
                 pl.semaphore_wait(ready.at[step, mark], 1)
 
         step, d = step + 1, 2 * d
+
+    for copy in index_copies:
+        copy.wait()
 
     def table(k, carry):
         found = [jnp.int32(0)] * cap
@@ -287,6 +301,7 @@
         for before in range(i):
             rank = rank + jnp.where(origins[before] == origins[i], 1, 0)
         mine_ref[i] = origins[i] * cap + jnp.minimum(rank, cap - 1)
+    mine_copy.start()
 
     def pass_halo_copy(n, at, j, low, size):
         ref = windows[at].at[n, halo_rows(low, size)]
@@ -645,6 +660,8 @@
 
     for n in range(shared):
         settle_kv(n)
+
+    mine_copy.wait()
 
     def drain(k, carry):
         for d in range(1, nh):
@@ -693,18 +710,18 @@
             jax.ShapeDtypeStruct((slots, BLK, heads * HD), query.dtype),
             jax.ShapeDtypeStruct((blocks,), jnp.int32),
         ],
-        in_specs=[pl.BlockSpec(memory_space=pltpu.SMEM)] * 2
-        + [pl.BlockSpec(memory_space=pltpu.HBM)] * 3,
-        out_specs=[
-            pl.BlockSpec(memory_space=pl.ANY),
-            pl.BlockSpec(memory_space=pltpu.SMEM),
-        ],
-        scratch_shapes=[pltpu.SMEM((slots,), jnp.int32)] * 2
+        in_specs=[pl.BlockSpec(memory_space=pltpu.HBM)] * 5,
+        out_specs=[pl.BlockSpec(memory_space=pl.ANY)] * 2,
+        scratch_shapes=[
+            pltpu.SMEM(n, jnp.int32)
+            for n in (doc_ids.shape, plan.shape, (blocks,), (slots,), (slots,))
+        ]
         + [pltpu.VMEM(shape, query.dtype) for shape in buffers]
         + [dma((heads, nh))] * 2
         + [dma((shared, 2, nh))] * 6
         + [dma((2, places, nh))] * 5
         + [dma((heads,))] * 4
+        + [dma((3,))]
         + [pltpu.SemaphoreType.REGULAR((nc.bit_length(), 2))],
         compiler_params=pltpu.CompilerParams(
             collective_id=0, has_side_effects=True, vmem_limit_bytes=held + (6 << 20)

time: 213 us -> 212 us (level)
  no operation moved by 1% of the time
where the time goes in v5:
time: 212 us
  Pallas kernels  212 us (100%)
    pallas_call x1, Pallas kernels, fused(): pl.pallas_call(functools.partial(fused_kernel, kv_heads, cap), out_shape=...  208 us

profile of v5, /device:TPU:21, one launch (start us, length us, event | category | flops | bytes accessed | tf_op | source)
XLA Modules:
  0.0 211.6 jit_solution(18069787017730333668)
XLA Ops:
  0.0 207.6 %fused.1 = (bf16[16,128,2048]{2,1,0:T(8,128)(2,1)S(1)}, s32[16]{0:T(128)S(1)}) custom-call(s32[128]{0:T(128)} %doc_hbm.1, s32[128]{0:T(128)} %plan_hbm.1, bf16[512,8192]{1,0:T(8,128)(2,1)} %q_ref.1, bf16[512,1024]{1,0:T(8,128)(2,1)} %k_ref.1, bf16[512,1024]{1,0:T(8,128)(2,1)} %v_ref.1), custom_call_target="tpu_custom_call" | custom-call | tf_op jit(solution)/shard_map/fused/pallas_call | solution.py:707
  207.6 4.0 %place.1 = bf16[2048,2048]{1,0:T(8,128)(2,1)} custom-call(s32[16]{0:T(128)S(1)} %get-tuple-element.7.mine_ref, bf16[16,128,2048]{2,1,0:T(8,128)(2,1)S(1)} %get-tuple-element.8.got_ref), custom_call_target="tpu_custom_call" | custom-call | tf_op jit(solution)/shard_map/place/pallas_call | solution.py:748

commit v6 on v5

--- a/solution.py
+++ b/solution.py
@@ -477,6 +477,9 @@
         jnp.int32, (BLK, BLK), 0
     )
 
+    def side_columns(k):
+        return pl.ds(aligned(lax.rem(k, 2) * HD), HD)
+
     def attend(k, slot):
         block = slot_block[slot]
         count = slot_count[slot]
@@ -494,7 +497,7 @@
         total = jnp.sum(functools.reduce(jnp.add, parts), axis=1, keepdims=True)
         weights = jnp.concatenate([x.astype(jnp.bfloat16) for x in parts], axis=1)
         mixed = jnp.dot(weights, values, preferred_element_type=jnp.float32) / total
-        out[k, slot] = mixed.astype(out.dtype)
+        out[lax.div(k, 2), slot, :, side_columns(k)] = mixed.astype(out.dtype)
 
     def owner(k):
         return 2 * pair + lax.div(lax.div(k, half), kv_heads)
@@ -513,20 +516,34 @@
     def send_out(k, s):
         t = target_of(s)
         col = column(k)
-        pltpu.make_async_remote_copy(
-            src_ref=out.at[k, pl.ds(t * cap, cap)],
-            dst_ref=got_ref.at[pl.ds(c * cap, cap), :, columns(col)],
-            send_sem=out_sent.at[k],
-            recv_sem=out_got.at[col],
-            device_id=(t, owner(k)),
-            device_id_type=MESH,
-        ).start()
+        slots_of = pl.ds(t * cap, cap)
+
+        def send(src, where):
+            pltpu.make_async_remote_copy(
+                src_ref=src,
+                dst_ref=got_ref.at[pl.ds(c * cap, cap), :, where],
+                send_sem=out_sent.at[k],
+                recv_sem=out_got.at[col],
+                device_id=(t, owner(k)),
+                device_id_type=MESH,
+            ).start()
+
+        @pl.when(k < half)
+        def _():
+            send(out.at[lax.div(k, 2), slots_of, :, side_columns(k)], columns(col))
+
+        @pl.when((k >= half) & (lax.rem(k, 2) == 1))
+        def _():
+            send(out.at[lax.div(k, 2), slots_of], both_columns(col))
+
+    def both_columns(col):
+        return pl.ds(aligned((col - 1) * HD), 2 * HD)
 
     own_slots = pl.ds(c * cap, cap)
 
     def send_own(k):
         col = column(k)
-        src = out.at[k, own_slots]
+        src = out.at[lax.div(k, 2), own_slots, :, side_columns(k)]
         dst = got_ref.at[own_slots, :, columns(col)]
 
         @pl.when(owner(k) == h)
@@ -669,11 +686,30 @@
 
         @pl.when(owner(k) != h)
         def _():
-            wait_on(out.at[k, own_slots], own_sent.at[k])
-
-        wait_on(out.at[k, pl.ds(0, (nc - 1) * cap)], out_sent.at[k])
+            wait_on(out.at[lax.div(k, 2), own_slots, :, side_columns(k)], own_sent.at[k])
+
         wait_on(got_ref.at[own_slots, :, columns(k)], own_got.at[k])
-        wait_on(got_ref.at[pl.ds(0, (nc - 1) * cap), :, columns(k)], out_got.at[k])
+        others = pl.ds(0, (nc - 1) * cap)
+        paired = lax.rem(k, 2) == 1
+
+        @pl.when(k < half)
+        def _():
+            wait_on(out.at[lax.div(k, 2), others, :, side_columns(k)], out_sent.at[k])
+
+        @pl.when((k >= half) & paired)
+        def _():
+            wait_on(out.at[lax.div(k, 2), others], out_sent.at[k])
+
+        first_group = side * kv_heads + lax.div(k, 2 * half) == 0
+
+        @pl.when(first_group)
+        def _():
+            wait_on(got_ref.at[others, :, columns(k)], out_got.at[k])
+
+        @pl.when(jnp.logical_not(first_group) & paired)
+        def _():
+            wait_on(got_ref.at[others, :, both_columns(k)], out_got.at[k])
+
         return carry
 
     lax.fori_loop(0, heads, drain, 0)
@@ -701,7 +737,7 @@
         (blocks, BLK, HD),
         (window // BLK, HD, BLK),
         (window // BLK, BLK, HD),
-        (heads, slots, BLK, HD),
+        (heads // 2, slots, BLK, 2 * HD),
     ]
     held = 2 * sum(math.prod(shape) for shape in buffers)
     return pl.pallas_call(
@@ -736,7 +772,7 @@
         copy = pltpu.make_async_copy(
             got_ref.at[mine_ref[i]], o_ref.at[pl.ds(i * BLK, BLK)], sems.at[i]
         )
-        copy.start()
+        copy.start(priority=i % 2)
         copies.append(copy)
     for copy in copies:
         copy.wait()

time: 212 us -> 212 us (level)
  no operation moved by 1% of the time
where the time goes in v6:
time: 212 us
  Pallas kernels  212 us (100%)
    pallas_call x1, Pallas kernels, fused(): pl.pallas_call(functools.partial(fused_kernel, kv_heads, cap), out_shape=...  208 us

profile of v6, /device:TPU:21, one launch (start us, length us, event | category | flops | bytes accessed | tf_op | source)
XLA Modules:
  0.0 211.6 jit_solution(9031184511317747597)
XLA Ops:
  0.0 207.6 %fused.1 = (bf16[16,128,2048]{2,1,0:T(8,128)(2,1)S(1)}, s32[16]{0:T(128)S(1)}) custom-call(s32[128]{0:T(128)} %doc_hbm.1, s32[128]{0:T(128)} %plan_hbm.1, bf16[512,8192]{1,0:T(8,128)(2,1)} %q_ref.1, bf16[512,1024]{1,0:T(8,128)(2,1)} %k_ref.1, bf16[512,1024]{1,0:T(8,128)(2,1)} %v_ref.1), custom_call_target="tpu_custom_call" | custom-call | tf_op jit(solution)/shard_map/fused/pallas_call | solution.py:743
  207.6 4.0 %place.1 = bf16[2048,2048]{1,0:T(8,128)(2,1)} custom-call(s32[16]{0:T(128)S(1)} %get-tuple-element.7.mine_ref, bf16[16,128,2048]{2,1,0:T(8,128)(2,1)S(1)} %get-tuple-element.8.got_ref), custom_call_target="tpu_custom_call" | custom-call | tf_op jit(solution)/shard_map/place/pallas_call | solution.py:784
